TPU v7x, 32 devices: a whole 2x2x4 slice. The times are simulated.
32 devices in a mesh: groups: 2 (over y), patch: 4 (over z), sub: 2 (over x), half: 2 (over core).
Axes of the slice: x: 2, y: 2, z: 4, core: 2. Of those that a mesh axis runs over, the one named last changes fastest.
Arguments:
- vectors: float32 [2, 8192, 256], P(None, ('groups', 'patch', 'sub', 'half')), parts along dimension 1, may hold values from -600 to 600
- prestress: bfloat16 [8192, 3, 256], P(('groups', 'patch', 'sub', 'half')), parts along dimension 0, may hold values from -4 to 4
- thickness: float32 [8192, 256], P(('groups', 'patch', 'sub', 'half')), parts along dimension 0, may hold values from 0.5 to 2
- foundation: float32 [8192, 256], P(('groups', 'patch', 'sub', 'half')), parts along dimension 0, may hold values from 2 to 6
- patch_rows: int32 [64], P(('groups', 'patch', 'sub', 'half')), parts along dimension 0, may hold values from 64 to 128, as said below
- matched: int32 [64], P(('groups', 'patch', 'sub', 'half')), parts along dimension 0, may hold values from 0 to 31, as said below
- elem_row: int32 [8192], P(('groups', 'patch', 'sub', 'half')), parts along dimension 0, may hold values from 0 to 4095, as said below
Outputs:
- modes: float32 [2, 8192, 256], P(None, ('groups', 'patch', 'sub', 'half')), parts along dimension 1
There are 2 independent parts, one for each index of `groups`. A program takes and returns all parts, laid end to end along the dimension named above; each array names one. Nothing has to cross between parts.
Inputs may be any that keep to these rules, and one draw needn't show every extreme that they name: `patch_rows`: the largest value is reached by some patch in every draw. A permutation of the patches; the patch matched to a patch lies on the device with the same sub and half indices and a patch index one above or one below, cyclically. `elem_row`: a permutation of the rows; of each device's rows, those in positions k * 16 to (k + 1) * 16 - 1 belong to patches of the device with index k along patch+sub+half.
All inputs are finite; a program needn't handle non-finite values.
Results may differ from a plain program's by a relative error of at most 0.0003.
Values may be sent and summed in bfloat16 or wider, within the bound.
A program may use at most 64 MiB of HBM per device.

v0:
```python
import jax
import jax.numpy as jnp
from jax import lax
from jax.sharding import PartitionSpec as P

ITERS = 2
step_size = 1.0
norm_scale = 16.0
penalty_value = 8.0
penalty_slope = 4.0


def passed_along(array, axis, by):
    peers = lax.axis_size(axis)
    return lax.ppermute(array, axis, [(i, (i + by) % peers) for i in range(peers)])


def second_rows(field):
    padded = jnp.pad(field, [(0, 0)] * (field.ndim - 2) + [(1, 1), (0, 0)])
    return padded[..., :-2, :] - 2.0 * field + padded[..., 2:, :]


def second_cols(field):
    padded = jnp.pad(field, [(0, 0)] * (field.ndim - 1) + [(1, 1)])
    return padded[..., :-2] - 2.0 * field + padded[..., 2:]


def forward_rows(field):
    zeros = jnp.zeros_like(field[..., :1, :])
    return jnp.concatenate([field[..., 1:, :], zeros], axis=-2) - field


def backward_rows(field):
    zeros = jnp.zeros_like(field[..., :1, :])
    return jnp.concatenate([zeros, field[..., :-1, :]], axis=-2) - field


def forward_cols(field):
    zeros = jnp.zeros_like(field[..., :1])
    return jnp.concatenate([field[..., 1:], zeros], axis=-1) - field


def backward_cols(field):
    zeros = jnp.zeros_like(field[..., :1])
    return jnp.concatenate([zeros, field[..., :-1]], axis=-1) - field


def stiffness(field, live, thickness, foundation):
    bend_rows = thickness * live * second_rows(field)
    bend_cols = thickness * second_cols(field)
    return live * (foundation * field + second_rows(bend_rows) + second_cols(bend_cols))


def geometric(field, live, stress):
    along_rows = forward_rows(field)
    along_cols = forward_cols(field)
    nuu = stress[:, :, 0, :]
    nvv = stress[:, :, 1, :]
    nuv = stress[:, :, 2, :]
    total = backward_rows(nuu * along_rows + nuv * along_cols) + backward_cols(
        nvv * along_cols + nuv * along_rows
    )
    return live * total


def edges(field, lengths):

    def row_pick(index):
        where_rows = jnp.broadcast_to(
            index[None, :, None, None], (field.shape[0], field.shape[1], 1, field.shape[3])
        )
        return jnp.take_along_axis(field, where_rows, axis=2)[:, :, 0, :]

    top = jnp.stack([row_pick(lengths - 2), row_pick(lengths - 1)], axis=2)
    bottom = field[:, :, 0:2, :]
    return (top, bottom)


def interface(field, lengths, top, bottom, partner_top, partner_bottom):
    jump_top = top[:, :, 1, :] - partner_bottom[:, :, 0, :]
    slope_top = (
        top[:, :, 1, :]
        - top[:, :, 0, :]
        - (partner_bottom[:, :, 1, :] - partner_bottom[:, :, 0, :])
    )
    jump_bottom = partner_top[:, :, 1, :] - bottom[:, :, 0, :]
    slope_bottom = (
        partner_top[:, :, 1, :]
        - partner_top[:, :, 0, :]
        - (bottom[:, :, 1, :] - bottom[:, :, 0, :])
    )
    rows = jnp.arange(field.shape[2], dtype=jnp.int32)[None, :, None]
    last = lengths[:, None, None] - 1
    added = jnp.where(
        rows == last, (penalty_value * jump_top + penalty_slope * slope_top)[:, :, None, :], 0.0
    )
    added = added + jnp.where(rows == last - 1, (-penalty_slope * slope_top)[:, :, None, :], 0.0)
    added = added + jnp.where(
        rows == 0, (-penalty_value * jump_bottom + penalty_slope * slope_bottom)[:, :, None, :], 0.0
    )
    added = added + jnp.where(rows == 1, (-penalty_slope * slope_bottom)[:, :, None, :], 0.0)
    return added


def products(field, kfield, gfield):
    return jnp.stack(
        [
            jnp.sum(field[0] * kfield[0]),
            jnp.sum(field[0] * kfield[1]),
            jnp.sum(field[1] * kfield[1]),
            jnp.sum(field[0] * gfield[0]),
            jnp.sum(field[0] * gfield[1]),
            jnp.sum(field[1] * gfield[1]),
        ]
    )


def advance(field, kfield, gfield, totals, precond, cells):
    first_a = totals[0]
    cross_k = totals[1]
    second_a = totals[2]
    first_g = totals[3]
    cross_g = totals[4]
    second_g = totals[5]
    ratio = cross_k / first_a
    other = field[1] - ratio * field[0]
    other_k = kfield[1] - ratio * kfield[0]
    other_g = gfield[1] - ratio * gfield[0]
    other_a = second_a - ratio * cross_k
    other_q = second_g - 2.0 * ratio * cross_g + ratio * ratio * first_g
    first_mu = first_g / first_a
    other_mu = other_q / other_a
    new_first = (field[0] + step_size * precond * (gfield[0] - first_mu * kfield[0])) * jnp.sqrt(
        norm_scale * cells / first_a
    )
    new_other = (other + step_size * precond * (other_g - other_mu * other_k)) * jnp.sqrt(
        norm_scale * cells / other_a
    )
    return jnp.stack([new_first, new_other])


def choose(candidates, wanted, labels):
    match = labels[None, :] == wanted[:, None]
    return jnp.sum(jnp.where(match[None, :, :, None, None], candidates[:, None], 0.0), axis=2)


def per_device(vectors, prestress, thickness, foundation, patch_rows, matched, elem_row):
    owners = lax.axis_size("patch")
    inner = lax.axis_size(("sub", "half"))
    slots = patch_rows.shape[0]
    rows_dev = thickness.shape[0]
    prows = rows_dev // slots
    ncol = thickness.shape[1]
    per_peer = rows_dev // (owners * inner)
    blocks = prestress.reshape(owners, inner, per_peer, 3, ncol)
    targets = (elem_row % rows_dev).reshape(owners, inner, per_peer)
    arrived, arrived_rows = (
        lax.all_to_all(
            lax.all_to_all(blocks, "patch", split_axis=0, concat_axis=0, tiled=True),
            ("sub", "half"),
            split_axis=1,
            concat_axis=1,
            tiled=True,
        ),
        lax.all_to_all(
            lax.all_to_all(targets, "patch", split_axis=0, concat_axis=0, tiled=True),
            ("sub", "half"),
            split_axis=1,
            concat_axis=1,
            tiled=True,
        ),
    )
    placed = (
        jnp.zeros((rows_dev, 3, ncol), jnp.bfloat16)
        .at[arrived_rows.reshape(-1)]
        .set(arrived.reshape(-1, 3, ncol))
    )
    stress = placed.astype(jnp.float32).reshape(slots, prows, 3, ncol)
    rows = jnp.arange(prows, dtype=jnp.int32)[None, :]
    live = (rows < patch_rows[:, None]).astype(jnp.float32)[:, :, None]
    thick = thickness.reshape(slots, prows, ncol)
    support = foundation.reshape(slots, prows, ncol)
    precond = live / (support + 12.0 * thick)
    own_ids = lax.axis_index(("patch", "sub", "half")) * slots + jnp.arange(slots, dtype=jnp.int32)
    labels = jnp.stack([own_ids, matched])
    field = vectors.reshape(2, slots, prows, ncol) * live
    cells = jnp.float32(owners * inner * rows_dev * ncol)
    for step in range(ITERS):
        top, bottom = edges(field, patch_rows)
        strips = jnp.stack([top, bottom])
        below = passed_along((strips, labels), "patch", 1)
        above = passed_along((strips, labels), "patch", -1)
        got_strips = jnp.stack([below[0], above[0]])
        got_labels = jnp.stack([below[1], above[1]])
        count = got_strips.shape[0] * slots
        cand_top = jnp.moveaxis(got_strips[:, 0], 0, 1).reshape(2, count, 2, ncol)
        cand_bottom = jnp.moveaxis(got_strips[:, 1], 0, 1).reshape(2, count, 2, ncol)
        cand_ids = got_labels[:, 0].reshape(-1)
        cand_next = got_labels[:, 1].reshape(-1)
        partner_bottom = choose(cand_bottom, matched, cand_ids)
        partner_top = choose(cand_top, own_ids, cand_next)
        kfield = stiffness(field, live, thick, support) + interface(
            field, patch_rows, top, bottom, partner_top, partner_bottom
        )
        gfield = geometric(field, live, stress)
        totals = lax.psum(products(field, kfield, gfield), ("patch", "sub", "half"))
        field = advance(field, kfield, gfield, totals, precond, cells)
    return field.reshape(2, rows_dev, ncol)


def solution(mesh):
    in_specs = (
        P(None, ("groups", "patch", "sub", "half"), None),
        P(("groups", "patch", "sub", "half"), None, None),
        P(("groups", "patch", "sub", "half"), None),
        P(("groups", "patch", "sub", "half"), None),
        P(("groups", "patch", "sub", "half")),
        P(("groups", "patch", "sub", "half")),
        P(("groups", "patch", "sub", "half")),
    )
    out_specs = P(None, ("groups", "patch", "sub", "half"), None)
    return jax.shard_map(
        per_device, mesh=mesh, in_specs=in_specs, out_specs=out_specs, check_vma=False
    )
```

profile of v0, /device:TPU:0, one launch (start us, length us, event | category | flops | bytes accessed | tf_op | source)
XLA Modules:
  0.0 211.1 jit_solution(15988298672852159609)
XLA Ops:
  1.1 1.1 broadcast_multiply_fusion
  2.2 12.3 %gather_fusion = f32[1024]{0:T(1024)S(1)} fusion(f32[2,2,128,256]{3,2,1,0:T(8,128)S(1)} %broadcast_multiply_fusion, s32[1024]{0:T(1024)S(1)} %bitcast.210), kind=kCustom, calls=%fused_computation.clone | custom fusion | bytes 24576 | tf_op jit(solution)/shard_map/jit(take_along_axis)/gather | solution.py:72
  14.6 12.3 %gather_fusion.1 = f32[1024]{0:T(1024)S(1)} fusion(f32[2,2,128,256]{3,2,1,0:T(8,128)S(1)} %broadcast_multiply_fusion, s32[1024]{0:T(1024)S(1)} %bitcast.212), kind=kCustom, calls=%fused_computation.1.clone | custom fusion | bytes 24576 | tf_op jit(solution)/shard_map/jit(take_along_axis)/gather | solution.py:72
  27.1 3.1 %collective-permute-start.2 = (f32[2,2,2,2,256]{4,3,2,1,0:T(2,128)S(1)}, f32[2,2,2,2,256]{4,3,2,1,0:T(2,128)S(1)}, u32[]{:S(2)}, u32[]{:S(2)}) collective-permute-start(f32[2,2,2,2,256]{4,3,2,1,0:T(2,128)S(1)} %pad_maximum_fusion.4), channel_id=1, source_target_pairs={{0,4},{4,8},{8,12},{12,0},{1,5},{5,9},{9,13},{13,1},{2,6},{6,10},{... | collective-permute-start | bytes 49160 | tf_op jit(solution)/shard_map/ppermute | solution.py:15
  30.1 2.1 collective-permute-start.3
  33.0 3.8 %collective-permute-start.1 = (s32[2,2]{1,0:T(2,128)S(1)}, s32[2,2]{1,0:T(2,128)S(1)}, u32[]{:S(2)}, u32[]{:S(2)}) collective-permute-start(s32[2,2]{1,0:T(2,128)S(1)} %pad_add_fusion.4), channel_id=1, source_target_pairs={{0,12},{4,0},{8,4},{12,8},{1,13},{5,1},{9,5},{13,9},{2,14},{6,2},{... | collective-permute-start | bytes 56 | tf_op jit(solution)/shard_map/ppermute | solution.py:15
  37.5 3.2 %all-to-all-start = ((s32[4,4,16]{2,1,0:T(4,128)}), s32[4,4,16]{2,1,0:T(4,128)S(1)}, u32[]{:S(2)}, u32[]{:S(2)}) async-start(s32[4,4,16]{2,1,0:T(4,128)} %reshape.291), calls=%async_computation | async-start | bytes 16384 | tf_op jit(solution)/shard_map/all_to_all | solution.py:166
  43.8 2.4 %all-to-all-done = s32[4,4,16]{2,1,0:T(4,128)S(1)} async-done(((s32[4,4,16]{2,1,0:T(4,128)}), s32[4,4,16]{2,1,0:T(4,128)S(1)}, u32[]{:S(2)}, u32[]{:S(2)}) %all-to-all-start) | async-done | bytes 1056 | tf_op jit(solution)/shard_map/all_to_all | solution.py:166
  46.9 3.2 %all-to-all-start.1 = ((s32[4,4,16]{2,0,1:T(4,128)}), s32[4,4,16]{2,0,1:T(4,128)S(1)}, u32[]{:S(2)}, u32[]{:S(2)}) async-start(s32[4,4,16]{2,0,1:T(4,128)} %copy.28), calls=%async_computation.1 | async-start | bytes 16384 | tf_op jit(solution)/shard_map/all_to_all | solution.py:165
  50.2 3.7 %all-to-all-done.1 = s32[4,4,16]{2,0,1:T(4,128)S(1)} async-done(((s32[4,4,16]{2,0,1:T(4,128)}), s32[4,4,16]{2,0,1:T(4,128)S(1)}, u32[]{:S(2)}, u32[]{:S(2)}) %all-to-all-start.1) | async-done | bytes 1056 | tf_op jit(solution)/shard_map/all_to_all | solution.py:165
  53.9 3.5 %all-to-all-start.2 = ((bf16[4,4,16,3,256]{4,2,1,3,0:T(8,128)(2,1)}), bf16[4,4,16,3,256]{4,2,1,3,0:T(8,128)(2,1)S(1)}, u32[]{:S(2)}, u32[]{:S(2)}) async-start(bf16[4,4,16,3,256]{4,2,1,3,0:T(8,128)(2,1)} %copy.30), calls=%async_computation.2 | async-start | bytes 786432 | tf_op jit(solution)/shard_map/all_to_all | solution.py:159
  57.8 11.4 %all-to-all-done.2 = bf16[4,4,16,3,256]{4,2,1,3,0:T(8,128)(2,1)S(1)} async-done(((bf16[4,4,16,3,256]{4,2,1,3,0:T(8,128)(2,1)}), bf16[4,4,16,3,256]{4,2,1,3,0:T(8,128)(2,1)S(1)}, u32[]{:S(2)}, u32[]{:S(2)}) %all-to-all-start.2) | async-done | bytes 393248 | tf_op jit(solution)/shard_map/all_to_all | solution.py:159
  70.0 3.5 %all-to-all-start.3 = ((bf16[4,4,16,3,256]{4,2,0,3,1:T(8,128)(2,1)}), bf16[4,4,16,3,256]{4,2,0,3,1:T(8,128)(2,1)S(1)}, u32[]{:S(2)}, u32[]{:S(2)}) async-start(bf16[4,4,16,3,256]{4,2,0,3,1:T(8,128)(2,1)} %copy.31), calls=%async_computation.3 | async-start | bytes 786432 | tf_op jit(solution)/shard_map/all_to_all | solution.py:158
  73.6 7.3 %all-to-all-done.3 = bf16[4,4,16,3,256]{4,2,0,3,1:T(8,128)(2,1)S(1)} async-done(((bf16[4,4,16,3,256]{4,2,0,3,1:T(8,128)(2,1)}), bf16[4,4,16,3,256]{4,2,0,3,1:T(8,128)(2,1)S(1)}, u32[]{:S(2)}, u32[]{:S(2)}) %all-to-all-start.3) | async-done | bytes 393248 | tf_op jit(solution)/shard_map/all_to_all | solution.py:158
  81.4 7.0 %scatter_fusion = bf16[256,3,256]{2,1,0:T(4,128)(2,1)S(1)} fusion(bf16[256,3,256]{2,1,0:T(4,128)(2,1)S(1)} %broadcast_in_dim.225, s32[256]{0:T(256)S(1)} %bitcast.260, bf16[256,3,256]{2,1,0:T(4,128)(2,1)S(1)} %copy.33), kind=kCustom, calls=%fused_computation.4 | custom fusion | bytes 1180672 | tf_op jit(solution)/shard_map/scatter | solution.py:176
  89.1 1.2 copy-done.7
  93.0 3.8 %stack.135 = f32[6]{0:T(128)S(1)} concatenate(f32[1]{0:T(128)} %bitcast.30, f32[1]{0:T(128)} %bitcast.32, f32[1]{0:T(128)} %bitcast.34, f32[1]{0:T(128)} %bitcast.36, f32[1]{0:T(128)} %bitcast.38, f32[1]{0:T(128)} %bitcast.39), dimensions={0} | concatenate | bytes 48 | tf_op jit(solution)/shard_map/stack | solution.py:106
  96.8 30.2 %psum.14 = f32[6]{0:T(128)S(1)} all-reduce(f32[6]{0:T(128)S(1)} %stack.135), channel_id=1, replica_groups=mesh['groups'=2,'patch'=4,'sub'=2,'half'=2] {'patch','sub','half'}, use_global_device_ids=true, to_apply=%region_9.11 | all-reduce | flops 6 | bytes 48 | tf_op jit(solution)/shard_map/psum | solution.py:206
  136.7 12.3 %gather_fusion.3 = f32[1024]{0:T(1024)S(1)} fusion(f32[2,2,128,256]{3,2,1,0:T(8,128)S(1)} %get-tuple-element.46, s32[1024]{0:T(1024)S(1)} %bitcast.213), kind=kCustom, calls=%fused_computation.3.clone | custom fusion | bytes 24576 | tf_op jit(solution)/shard_map/jit(take_along_axis)/gather | solution.py:72
  149.1 12.3 %gather_fusion.2 = f32[1024]{0:T(1024)S(1)} fusion(f32[2,2,128,256]{3,2,1,0:T(8,128)S(1)} %get-tuple-element.46, s32[1024]{0:T(1024)S(1)} %bitcast.211), kind=kCustom, calls=%fused_computation.2.clone | custom fusion | bytes 24576 | tf_op jit(solution)/shard_map/jit(take_along_axis)/gather | solution.py:72
  161.6 3.8 %collective-permute-start.5 = (f32[2,2,2,2,256]{4,3,2,1,0:T(2,128)S(1)}, f32[2,2,2,2,256]{4,3,2,1,0:T(2,128)S(1)}, u32[]{:S(2)}, u32[]{:S(2)}) collective-permute-start(f32[2,2,2,2,256]{4,3,2,1,0:T(2,128)S(1)} %pad_maximum_fusion.5), channel_id=1, source_target_pairs={{0,12},{4,0},{8,4},{12,8},{1,13},{5,1},{9,5},{13,9},{2,14},{6,2},{... | collective-permute-start | bytes 49160 | tf_op jit(solution)/shard_map/ppermute | solution.py:15
  166.1 1.1 collective-permute-done.4
  169.5 3.8 %stack.150 = f32[6]{0:T(128)S(1)} concatenate(f32[1]{0:T(128)} %bitcast.59, f32[1]{0:T(128)} %bitcast.61, f32[1]{0:T(128)} %bitcast.62, f32[1]{0:T(128)} %bitcast.64, f32[1]{0:T(128)} %bitcast.66, f32[1]{0:T(128)} %bitcast.67), dimensions={0} | concatenate | bytes 48 | tf_op jit(solution)/shard_map/stack | solution.py:106
  173.4 29.5 %psum.15 = f32[6]{0:T(128)S(1)} all-reduce(f32[6]{0:T(128)S(1)} %stack.150), channel_id=1, replica_groups=mesh['groups'=2,'patch'=4,'sub'=2,'half'=2] {'patch','sub','half'}, use_global_device_ids=true, to_apply=%region_18.20 | all-reduce | flops 6 | bytes 48 | tf_op jit(solution)/shard_map/psum | solution.py:206
  (130 shorter events, 19.5 us)
Async XLA Ops:
  0.0 0.7 copy-start.12
  27.1 30.4 %collective-permute-start.2 = (f32[2,2,2,2,256]{4,3,2,1,0:T(2,128)S(1)}, f32[2,2,2,2,256]{4,3,2,1,0:T(2,128)S(1)}, u32[]{:S(2)}, u32[]{:S(2)}) collective-permute-start(f32[2,2,2,2,256]{4,3,2,1,0:T(2,128)S(1)} %pad_maximum_fusion.4), channel_id=1, source_target_pairs={{0,4},{4,8},{8,12},{12,0},{1,5},{5,9},{9,13},{13,1},{2,6},{6,10},{... | collective-permute-start | bytes 49160 | tf_op jit(solution)/shard_map/ppermute | solution.py:15
  30.1 27.3 %collective-permute-start.3 = (f32[2,2,2,2,256]{4,3,2,1,0:T(2,128)S(1)}, f32[2,2,2,2,256]{4,3,2,1,0:T(2,128)S(1)}, u32[]{:S(2)}, u32[]{:S(2)}) collective-permute-start(f32[2,2,2,2,256]{4,3,2,1,0:T(2,128)S(1)} %pad_maximum_fusion.4), channel_id=1, source_target_pairs={{0,12},{4,0},{8,4},{12,8},{1,13},{5,1},{9,5},{13,9},{2,14},{6,2},{... | collective-permute-start | bytes 49160 | tf_op jit(solution)/shard_map/ppermute | solution.py:15
  32.2 0.7 copy-start.13
  32.9 3.9 %copy-start.11 = (s32[256]{0:T(256)S(1)}, s32[256]{0:T(256)}, u32[]{:S(2)}) copy-start(s32[256]{0:T(256)} %param.15) | copy-start | bytes 3076
  32.9 10.7 %collective-permute-start = (s32[2,2]{1,0:T(2,128)S(1)}, s32[2,2]{1,0:T(2,128)S(1)}, u32[]{:S(2)}, u32[]{:S(2)}) collective-permute-start(s32[2,2]{1,0:T(2,128)S(1)} %pad_add_fusion.4), channel_id=1, source_target_pairs={{0,4},{4,8},{8,12},{12,0},{1,5},{5,9},{9,13},{13,1},{2,6},{6,10},{... | collective-permute-start | bytes 56 | tf_op jit(solution)/shard_map/ppermute | solution.py:15
  33.0 10.6 %collective-permute-start.1 = (s32[2,2]{1,0:T(2,128)S(1)}, s32[2,2]{1,0:T(2,128)S(1)}, u32[]{:S(2)}, u32[]{:S(2)}) collective-permute-start(s32[2,2]{1,0:T(2,128)S(1)} %pad_add_fusion.4), channel_id=1, source_target_pairs={{0,12},{4,0},{8,4},{12,8},{1,13},{5,1},{9,5},{13,9},{2,14},{6,2},{... | collective-permute-start | bytes 56 | tf_op jit(solution)/shard_map/ppermute | solution.py:15
  37.5 8.8 %all-to-all-start = ((s32[4,4,16]{2,1,0:T(4,128)}), s32[4,4,16]{2,1,0:T(4,128)S(1)}, u32[]{:S(2)}, u32[]{:S(2)}) async-start(s32[4,4,16]{2,1,0:T(4,128)} %reshape.291), calls=%async_computation | async-start | bytes 16384 | tf_op jit(solution)/shard_map/all_to_all | solution.py:166
  40.8 1.1 copy-start
  41.8 1.0 copy-start.10
  46.9 7.0 %all-to-all-start.1 = ((s32[4,4,16]{2,0,1:T(4,128)}), s32[4,4,16]{2,0,1:T(4,128)S(1)}, u32[]{:S(2)}, u32[]{:S(2)}) async-start(s32[4,4,16]{2,0,1:T(4,128)} %copy.28), calls=%async_computation.1 | async-start | bytes 16384 | tf_op jit(solution)/shard_map/all_to_all | solution.py:165
  53.9 15.4 %all-to-all-start.2 = ((bf16[4,4,16,3,256]{4,2,1,3,0:T(8,128)(2,1)}), bf16[4,4,16,3,256]{4,2,1,3,0:T(8,128)(2,1)S(1)}, u32[]{:S(2)}, u32[]{:S(2)}) async-start(bf16[4,4,16,3,256]{4,2,1,3,0:T(8,128)(2,1)} %copy.30), calls=%async_computation.2 | async-start | bytes 786432 | tf_op jit(solution)/shard_map/all_to_all | solution.py:159
  70.0 10.9 %all-to-all-start.3 = ((bf16[4,4,16,3,256]{4,2,0,3,1:T(8,128)(2,1)}), bf16[4,4,16,3,256]{4,2,0,3,1:T(8,128)(2,1)S(1)}, u32[]{:S(2)}, u32[]{:S(2)}) async-start(bf16[4,4,16,3,256]{4,2,0,3,1:T(8,128)(2,1)} %copy.31), calls=%async_computation.3 | async-start | bytes 786432 | tf_op jit(solution)/shard_map/all_to_all | solution.py:158
  89.0 1.2 copy-start.7
  89.0 1.6 copy-start.2
  89.0 1.6 copy-start.4
  90.2 0.9 copy-start.1
  90.2 1.1 copy-start.6
  135.5 1.0 copy-start.3
  135.5 1.0 copy-start.5
  161.6 5.6 %collective-permute-start.4 = (f32[2,2,2,2,256]{4,3,2,1,0:T(2,128)S(1)}, f32[2,2,2,2,256]{4,3,2,1,0:T(2,128)S(1)}, u32[]{:S(2)}, u32[]{:S(2)}) collective-permute-start(f32[2,2,2,2,256]{4,3,2,1,0:T(2,128)S(1)} %pad_maximum_fusion.5), channel_id=1, source_target_pairs={{0,4},{4,8},{8,12},{12,0},{1,5},{5,9},{9,13},{13,1},{2,6},{6,10},{... | collective-permute-start | bytes 49160 | tf_op jit(solution)/shard_map/ppermute | solution.py:15
  161.6 5.5 %collective-permute-start.5 = (f32[2,2,2,2,256]{4,3,2,1,0:T(2,128)S(1)}, f32[2,2,2,2,256]{4,3,2,1,0:T(2,128)S(1)}, u32[]{:S(2)}, u32[]{:S(2)}) collective-permute-start(f32[2,2,2,2,256]{4,3,2,1,0:T(2,128)S(1)} %pad_maximum_fusion.5), channel_id=1, source_target_pairs={{0,12},{4,0},{8,4},{12,8},{1,13},{5,1},{9,5},{13,9},{2,14},{6,2},{... | collective-permute-start | bytes 49160 | tf_op jit(solution)/shard_map/ppermute | solution.py:15
  167.6 1.0 copy-start.8
  167.7 1.0 copy-start.9
where the time goes:
time: 212 us; the launch traced here: 211 us
  local copies, waits for them, and re-layouts  75.2 us (35%)
  blocking collectives  59.7 us (28%)
  starting transfers between devices  26.3 us (12%)
  waiting for transfers between devices  26 us (12%)
  between operations  13.6 us (6%)
  other arithmetic  10.3 us (5%)
    psum x2, blocking collectives, per_device(): totals = lax.psum(products(field, kfield, gfield), ('patch', 'sub', 'half'))  59.7 us
    gather x4, local copies, waits for them, and re-layouts, row_pick(): return jnp.take_along_axis(field, where_rows, axis=2)[:, :, 0, :]  49.2 us
    ppermute x6, starting transfers between devices, passed_along(): lax.ppermute(array, axis, [(i, (i + by) % peers) for i in range(peers)])  12.9 us
    all_to_all x1, waiting for transfers between devices, per_device(): lax.all_to_all(blocks, 'patch', split_axis=0, concat_axis=0, tiled=True)  11.4 us
    another operation x2, local copies, waits for them, and re-layouts, products(): jnp.stack([jnp.sum(field[0] * kfield[0]), jnp.sum(field[0] * kfield[1]),...  7.63 us
    all_to_all x1, waiting for transfers between devices, per_device(): lax.all_to_all(lax.all_to_all(blocks, 'patch', split_axis=0, concat_axis=...  7.33 us
    scatter x1, local copies, waits for them, and re-layouts, per_device(): placed = jnp.zeros((rows_dev, 3, ncol), jnp.bfloat16).at[arrived_rows.res...  6.97 us
    unnamed x40, local copies, waits for them, and re-layouts  4.77 us
  transfers between devices with their start and end apart: 10, of which 5 were waited for; matrix products, arithmetic and copies ran while one was open for 2% of the time, Pallas kernels for 0%

commit v1 on v0

--- a/solution.py
+++ b/solution.py
@@ -203,7 +203,7 @@
             field, patch_rows, top, bottom, partner_top, partner_bottom
         )
         gfield = geometric(field, live, stress)
-        totals = lax.psum(products(field, kfield, gfield), ("patch", "sub", "half"))
+        totals = lax.psum(lax.psum(products(field, kfield, gfield), ("sub", "half")), "patch")
         field = advance(field, kfield, gfield, totals, precond, cells)
     return field.reshape(2, rows_dev, ncol)
 

time: 212 us -> 186 us (0.88)
  blocking collectives: 59.7 us -> 33.4 us
    psum x2 -> x4, blocking collectives: 59.7 us -> 33.4 us  [the longest x2 22 us: per_device(): lax.psum(lax.psum(products(field, kfield, gfield), ('sub', 'half')), 'pat...]
  transfers between devices with their start and end apart: 10 -> 10, of which waited for: 5 -> 5; matrix products, arithmetic and copies ran while one was open for 2% -> 3% of each run, Pallas kernels for 0% -> 0%
where the time goes in v1:
time: 186 us; the launch traced here: 185 us
  local copies, waits for them, and re-layouts  75.2 us (40%)
  blocking collectives  33.4 us (18%)
  starting transfers between devices  26.3 us (14%)
  waiting for transfers between devices  26 us (14%)
  between operations  13.6 us (7%)
  other arithmetic  10.3 us (6%)
    gather x4, local copies, waits for them, and re-layouts, row_pick(): return jnp.take_along_axis(field, where_rows, axis=2)[:, :, 0, :]  49.2 us
    psum x2, blocking collectives, per_device(): lax.psum(lax.psum(products(field, kfield, gfield), ('sub', 'half')), 'pat...  22 us
    ppermute x6, starting transfers between devices, passed_along(): lax.ppermute(array, axis, [(i, (i + by) % peers) for i in range(peers)])  12.9 us
    all_to_all x1, waiting for transfers between devices, per_device(): lax.all_to_all(blocks, 'patch', split_axis=0, concat_axis=0, tiled=True)  11.4 us
    psum x2, blocking collectives, per_device(): lax.psum(products(field, kfield, gfield), ('sub', 'half'))  11.4 us
    another operation x2, local copies, waits for them, and re-layouts, products(): jnp.stack([jnp.sum(field[0] * kfield[0]), jnp.sum(field[0] * kfield[1]),...  7.63 us
    all_to_all x1, waiting for transfers between devices, per_device(): lax.all_to_all(lax.all_to_all(blocks, 'patch', split_axis=0, concat_axis=...  7.33 us
    scatter x1, local copies, waits for them, and re-layouts, per_device(): placed = jnp.zeros((rows_dev, 3, ncol), jnp.bfloat16).at[arrived_rows.res...  6.97 us
  transfers between devices with their start and end apart: 10, of which 5 were waited for; matrix products, arithmetic and copies ran while one was open for 3% of the time, Pallas kernels for 0%

profile of v1, /device:TPU:0, one launch (start us, length us, event | category | flops | bytes accessed | tf_op | source)
XLA Modules:
  0.0 184.7 jit_solution(1604891253393399544)
XLA Ops:
  2.2 12.3 %gather_fusion = f32[1024]{0:T(1024)S(1)} fusion(f32[2,2,128,256]{3,2,1,0:T(8,128)S(1)} %broadcast_multiply_fusion, s32[1024]{0:T(1024)S(1)} %bitcast.210), kind=kCustom, calls=%fused_computation.clone | custom fusion | bytes 24576 | tf_op jit(solution)/shard_map/jit(take_along_axis)/gather | solution.py:72
  14.6 12.3 %gather_fusion.1 = f32[1024]{0:T(1024)S(1)} fusion(f32[2,2,128,256]{3,2,1,0:T(8,128)S(1)} %broadcast_multiply_fusion, s32[1024]{0:T(1024)S(1)} %bitcast.212), kind=kCustom, calls=%fused_computation.1.clone | custom fusion | bytes 24576 | tf_op jit(solution)/shard_map/jit(take_along_axis)/gather | solution.py:72
  27.1 3.1 %collective-permute-start.2 = (f32[2,2,2,2,256]{4,3,2,1,0:T(2,128)S(1)}, f32[2,2,2,2,256]{4,3,2,1,0:T(2,128)S(1)}, u32[]{:S(2)}, u32[]{:S(2)}) collective-permute-start(f32[2,2,2,2,256]{4,3,2,1,0:T(2,128)S(1)} %pad_maximum_fusion.4), channel_id=1, source_target_pairs={{0,4},{4,8},{8,12},{12,0},{1,5},{5,9},{9,13},{13,1},{2,6},{6,10},{... | collective-permute-start | bytes 49160 | tf_op jit(solution)/shard_map/ppermute | solution.py:15
  30.1 2.1 %collective-permute-start.3 = (f32[2,2,2,2,256]{4,3,2,1,0:T(2,128)S(1)}, f32[2,2,2,2,256]{4,3,2,1,0:T(2,128)S(1)}, u32[]{:S(2)}, u32[]{:S(2)}) collective-permute-start(f32[2,2,2,2,256]{4,3,2,1,0:T(2,128)S(1)} %pad_maximum_fusion.4), channel_id=1, source_target_pairs={{0,12},{4,0},{8,4},{12,8},{1,13},{5,1},{9,5},{13,9},{2,14},{6,2},{... | collective-permute-start | bytes 49160 | tf_op jit(solution)/shard_map/ppermute | solution.py:15
  33.0 3.8 %collective-permute-start.1 = (s32[2,2]{1,0:T(2,128)S(1)}, s32[2,2]{1,0:T(2,128)S(1)}, u32[]{:S(2)}, u32[]{:S(2)}) collective-permute-start(s32[2,2]{1,0:T(2,128)S(1)} %pad_add_fusion.4), channel_id=1, source_target_pairs={{0,12},{4,0},{8,4},{12,8},{1,13},{5,1},{9,5},{13,9},{2,14},{6,2},{... | collective-permute-start | bytes 56 | tf_op jit(solution)/shard_map/ppermute | solution.py:15
  37.5 3.2 %all-to-all-start = ((s32[4,4,16]{2,1,0:T(4,128)}), s32[4,4,16]{2,1,0:T(4,128)S(1)}, u32[]{:S(2)}, u32[]{:S(2)}) async-start(s32[4,4,16]{2,1,0:T(4,128)} %reshape.291), calls=%async_computation | async-start | bytes 16384 | tf_op jit(solution)/shard_map/all_to_all | solution.py:166
  43.8 2.4 %all-to-all-done = s32[4,4,16]{2,1,0:T(4,128)S(1)} async-done(((s32[4,4,16]{2,1,0:T(4,128)}), s32[4,4,16]{2,1,0:T(4,128)S(1)}, u32[]{:S(2)}, u32[]{:S(2)}) %all-to-all-start) | async-done | bytes 1056 | tf_op jit(solution)/shard_map/all_to_all | solution.py:166
  46.9 3.2 %all-to-all-start.1 = ((s32[4,4,16]{2,0,1:T(4,128)}), s32[4,4,16]{2,0,1:T(4,128)S(1)}, u32[]{:S(2)}, u32[]{:S(2)}) async-start(s32[4,4,16]{2,0,1:T(4,128)} %copy.28), calls=%async_computation.1 | async-start | bytes 16384 | tf_op jit(solution)/shard_map/all_to_all | solution.py:165
  50.2 3.7 %all-to-all-done.1 = s32[4,4,16]{2,0,1:T(4,128)S(1)} async-done(((s32[4,4,16]{2,0,1:T(4,128)}), s32[4,4,16]{2,0,1:T(4,128)S(1)}, u32[]{:S(2)}, u32[]{:S(2)}) %all-to-all-start.1) | async-done | bytes 1056 | tf_op jit(solution)/shard_map/all_to_all | solution.py:165
  53.9 3.5 %all-to-all-start.2 = ((bf16[4,4,16,3,256]{4,2,1,3,0:T(8,128)(2,1)}), bf16[4,4,16,3,256]{4,2,1,3,0:T(8,128)(2,1)S(1)}, u32[]{:S(2)}, u32[]{:S(2)}) async-start(bf16[4,4,16,3,256]{4,2,1,3,0:T(8,128)(2,1)} %copy.30), calls=%async_computation.2 | async-start | bytes 786432 | tf_op jit(solution)/shard_map/all_to_all | solution.py:159
  57.8 11.4 %all-to-all-done.2 = bf16[4,4,16,3,256]{4,2,1,3,0:T(8,128)(2,1)S(1)} async-done(((bf16[4,4,16,3,256]{4,2,1,3,0:T(8,128)(2,1)}), bf16[4,4,16,3,256]{4,2,1,3,0:T(8,128)(2,1)S(1)}, u32[]{:S(2)}, u32[]{:S(2)}) %all-to-all-start.2) | async-done | bytes 393248 | tf_op jit(solution)/shard_map/all_to_all | solution.py:159
  70.0 3.5 %all-to-all-start.3 = ((bf16[4,4,16,3,256]{4,2,0,3,1:T(8,128)(2,1)}), bf16[4,4,16,3,256]{4,2,0,3,1:T(8,128)(2,1)S(1)}, u32[]{:S(2)}, u32[]{:S(2)}) async-start(bf16[4,4,16,3,256]{4,2,0,3,1:T(8,128)(2,1)} %copy.31), calls=%async_computation.3 | async-start | bytes 786432 | tf_op jit(solution)/shard_map/all_to_all | solution.py:158
  73.6 7.3 %all-to-all-done.3 = bf16[4,4,16,3,256]{4,2,0,3,1:T(8,128)(2,1)S(1)} async-done(((bf16[4,4,16,3,256]{4,2,0,3,1:T(8,128)(2,1)}), bf16[4,4,16,3,256]{4,2,0,3,1:T(8,128)(2,1)S(1)}, u32[]{:S(2)}, u32[]{:S(2)}) %all-to-all-start.3) | async-done | bytes 393248 | tf_op jit(solution)/shard_map/all_to_all | solution.py:158
  81.4 7.0 %scatter_fusion = bf16[256,3,256]{2,1,0:T(4,128)(2,1)S(1)} fusion(bf16[256,3,256]{2,1,0:T(4,128)(2,1)S(1)} %broadcast_in_dim.225, s32[256]{0:T(256)S(1)} %bitcast.260, bf16[256,3,256]{2,1,0:T(4,128)(2,1)S(1)} %copy.33), kind=kCustom, calls=%fused_computation.4 | custom fusion | bytes 1180672 | tf_op jit(solution)/shard_map/scatter | solution.py:176
  89.1 1.2 copy-done.7
  93.0 3.8 %stack.135 = f32[6]{0:T(128)S(1)} concatenate(f32[1]{0:T(128)} %bitcast.30, f32[1]{0:T(128)} %bitcast.32, f32[1]{0:T(128)} %bitcast.34, f32[1]{0:T(128)} %bitcast.36, f32[1]{0:T(128)} %bitcast.38, f32[1]{0:T(128)} %bitcast.39), dimensions={0} | concatenate | bytes 48 | tf_op jit(solution)/shard_map/stack | solution.py:106
  96.8 5.7 %psum.28 = f32[6]{0:T(128)S(1)} all-reduce(f32[6]{0:T(128)S(1)} %stack.135), channel_id=1, replica_groups=mesh['groups'=2,'patch'=4,'sub'=2,'half'=2] {'sub','half'}, use_global_device_ids=true, to_apply=%region_9.11 | all-reduce | flops 6 | bytes 48 | tf_op jit(solution)/shard_map/psum | solution.py:206
  102.6 9.8 %psum.29 = f32[6]{0:T(128)S(1)} all-reduce(f32[6]{0:T(128)S(1)} %psum.28), channel_id=1, replica_groups=mesh['groups'=2,'patch'=4,'sub'=2,'half'=2] {'patch'}, use_global_device_ids=true, to_apply=%region_10.12 | all-reduce | flops 6 | bytes 48 | tf_op jit(solution)/shard_map/psum | solution.py:206
  122.0 12.3 %gather_fusion.3 = f32[1024]{0:T(1024)S(1)} fusion(f32[2,2,128,256]{3,2,1,0:T(8,128)S(1)} %get-tuple-element.46, s32[1024]{0:T(1024)S(1)} %bitcast.213), kind=kCustom, calls=%fused_computation.3.clone | custom fusion | bytes 24576 | tf_op jit(solution)/shard_map/jit(take_along_axis)/gather | solution.py:72
  134.4 12.3 %gather_fusion.2 = f32[1024]{0:T(1024)S(1)} fusion(f32[2,2,128,256]{3,2,1,0:T(8,128)S(1)} %get-tuple-element.46, s32[1024]{0:T(1024)S(1)} %bitcast.211), kind=kCustom, calls=%fused_computation.2.clone | custom fusion | bytes 24576 | tf_op jit(solution)/shard_map/jit(take_along_axis)/gather | solution.py:72
  147.5 3.3 %collective-permute-start.5 = (f32[2,2,2,2,256]{4,3,2,1,0:T(2,128)S(1)}, f32[2,2,2,2,256]{4,3,2,1,0:T(2,128)S(1)}, u32[]{:S(2)}, u32[]{:S(2)}) collective-permute-start(f32[2,2,2,2,256]{4,3,2,1,0:T(2,128)S(1)} %pad_maximum_fusion.5), channel_id=1, source_target_pairs={{0,12},{4,0},{8,4},{12,8},{1,13},{5,1},{9,5},{13,9},{2,14},{6,2},{... | collective-permute-start | bytes 49160 | tf_op jit(solution)/shard_map/ppermute | solution.py:15
  154.8 3.8 %stack.150 = f32[6]{0:T(128)S(1)} concatenate(f32[1]{0:T(128)} %bitcast.59, f32[1]{0:T(128)} %bitcast.61, f32[1]{0:T(128)} %bitcast.62, f32[1]{0:T(128)} %bitcast.64, f32[1]{0:T(128)} %bitcast.66, f32[1]{0:T(128)} %bitcast.67), dimensions={0} | concatenate | bytes 48 | tf_op jit(solution)/shard_map/stack | solution.py:106
  158.7 5.6 %psum.30 = f32[6]{0:T(128)S(1)} all-reduce(f32[6]{0:T(128)S(1)} %stack.150), channel_id=1, replica_groups=mesh['groups'=2,'patch'=4,'sub'=2,'half'=2] {'sub','half'}, use_global_device_ids=true, to_apply=%region_19.21 | all-reduce | flops 6 | bytes 48 | tf_op jit(solution)/shard_map/psum | solution.py:206
  164.3 12.2 %psum.31 = f32[6]{0:T(128)S(1)} all-reduce(f32[6]{0:T(128)S(1)} %psum.30), channel_id=1, replica_groups=mesh['groups'=2,'patch'=4,'sub'=2,'half'=2] {'patch'}, use_global_device_ids=true, to_apply=%region_20.22 | all-reduce | flops 6 | bytes 48 | tf_op jit(solution)/shard_map/psum | solution.py:206
  (132 shorter events, 22.3 us)
Async XLA Ops:
  0.0 0.7 copy-start.12
  27.1 30.4 %collective-permute-start.2 = (f32[2,2,2,2,256]{4,3,2,1,0:T(2,128)S(1)}, f32[2,2,2,2,256]{4,3,2,1,0:T(2,128)S(1)}, u32[]{:S(2)}, u32[]{:S(2)}) collective-permute-start(f32[2,2,2,2,256]{4,3,2,1,0:T(2,128)S(1)} %pad_maximum_fusion.4), channel_id=1, source_target_pairs={{0,4},{4,8},{8,12},{12,0},{1,5},{5,9},{9,13},{13,1},{2,6},{6,10},{... | collective-permute-start | bytes 49160 | tf_op jit(solution)/shard_map/ppermute | solution.py:15
  30.1 27.3 %collective-permute-start.3 = (f32[2,2,2,2,256]{4,3,2,1,0:T(2,128)S(1)}, f32[2,2,2,2,256]{4,3,2,1,0:T(2,128)S(1)}, u32[]{:S(2)}, u32[]{:S(2)}) collective-permute-start(f32[2,2,2,2,256]{4,3,2,1,0:T(2,128)S(1)} %pad_maximum_fusion.4), channel_id=1, source_target_pairs={{0,12},{4,0},{8,4},{12,8},{1,13},{5,1},{9,5},{13,9},{2,14},{6,2},{... | collective-permute-start | bytes 49160 | tf_op jit(solution)/shard_map/ppermute | solution.py:15
  32.2 0.7 copy-start.13
  32.9 3.9 %copy-start.11 = (s32[256]{0:T(256)S(1)}, s32[256]{0:T(256)}, u32[]{:S(2)}) copy-start(s32[256]{0:T(256)} %param.15) | copy-start | bytes 3076
  32.9 10.7 %collective-permute-start = (s32[2,2]{1,0:T(2,128)S(1)}, s32[2,2]{1,0:T(2,128)S(1)}, u32[]{:S(2)}, u32[]{:S(2)}) collective-permute-start(s32[2,2]{1,0:T(2,128)S(1)} %pad_add_fusion.4), channel_id=1, source_target_pairs={{0,4},{4,8},{8,12},{12,0},{1,5},{5,9},{9,13},{13,1},{2,6},{6,10},{... | collective-permute-start | bytes 56 | tf_op jit(solution)/shard_map/ppermute | solution.py:15
  33.0 10.6 %collective-permute-start.1 = (s32[2,2]{1,0:T(2,128)S(1)}, s32[2,2]{1,0:T(2,128)S(1)}, u32[]{:S(2)}, u32[]{:S(2)}) collective-permute-start(s32[2,2]{1,0:T(2,128)S(1)} %pad_add_fusion.4), channel_id=1, source_target_pairs={{0,12},{4,0},{8,4},{12,8},{1,13},{5,1},{9,5},{13,9},{2,14},{6,2},{... | collective-permute-start | bytes 56 | tf_op jit(solution)/shard_map/ppermute | solution.py:15
  37.5 8.8 %all-to-all-start = ((s32[4,4,16]{2,1,0:T(4,128)}), s32[4,4,16]{2,1,0:T(4,128)S(1)}, u32[]{:S(2)}, u32[]{:S(2)}) async-start(s32[4,4,16]{2,1,0:T(4,128)} %reshape.291), calls=%async_computation | async-start | bytes 16384 | tf_op jit(solution)/shard_map/all_to_all | solution.py:166
  40.8 1.1 copy-start
  41.8 1.0 copy-start.10
  46.9 7.0 %all-to-all-start.1 = ((s32[4,4,16]{2,0,1:T(4,128)}), s32[4,4,16]{2,0,1:T(4,128)S(1)}, u32[]{:S(2)}, u32[]{:S(2)}) async-start(s32[4,4,16]{2,0,1:T(4,128)} %copy.28), calls=%async_computation.1 | async-start | bytes 16384 | tf_op jit(solution)/shard_map/all_to_all | solution.py:165
  53.9 15.4 %all-to-all-start.2 = ((bf16[4,4,16,3,256]{4,2,1,3,0:T(8,128)(2,1)}), bf16[4,4,16,3,256]{4,2,1,3,0:T(8,128)(2,1)S(1)}, u32[]{:S(2)}, u32[]{:S(2)}) async-start(bf16[4,4,16,3,256]{4,2,1,3,0:T(8,128)(2,1)} %copy.30), calls=%async_computation.2 | async-start | bytes 786432 | tf_op jit(solution)/shard_map/all_to_all | solution.py:159
  70.0 10.9 %all-to-all-start.3 = ((bf16[4,4,16,3,256]{4,2,0,3,1:T(8,128)(2,1)}), bf16[4,4,16,3,256]{4,2,0,3,1:T(8,128)(2,1)S(1)}, u32[]{:S(2)}, u32[]{:S(2)}) async-start(bf16[4,4,16,3,256]{4,2,0,3,1:T(8,128)(2,1)} %copy.31), calls=%async_computation.3 | async-start | bytes 786432 | tf_op jit(solution)/shard_map/all_to_all | solution.py:158
  89.0 1.2 copy-start.7
  89.0 1.6 copy-start.2
  89.0 1.6 copy-start.4
  90.2 0.9 copy-start.1
  90.2 1.1 copy-start.6
  120.8 1.0 copy-start.3
  120.8 1.0 copy-start.5
  146.9 5.6 %collective-permute-start.4 = (f32[2,2,2,2,256]{4,3,2,1,0:T(2,128)S(1)}, f32[2,2,2,2,256]{4,3,2,1,0:T(2,128)S(1)}, u32[]{:S(2)}, u32[]{:S(2)}) collective-permute-start(f32[2,2,2,2,256]{4,3,2,1,0:T(2,128)S(1)} %pad_maximum_fusion.5), channel_id=1, source_target_pairs={{0,4},{4,8},{8,12},{12,0},{1,5},{5,9},{9,13},{13,1},{2,6},{6,10},{... | collective-permute-start | bytes 49160 | tf_op jit(solution)/shard_map/ppermute | solution.py:15
  147.5 5.0 %collective-permute-start.5 = (f32[2,2,2,2,256]{4,3,2,1,0:T(2,128)S(1)}, f32[2,2,2,2,256]{4,3,2,1,0:T(2,128)S(1)}, u32[]{:S(2)}, u32[]{:S(2)}) collective-permute-start(f32[2,2,2,2,256]{4,3,2,1,0:T(2,128)S(1)} %pad_maximum_fusion.5), channel_id=1, source_target_pairs={{0,12},{4,0},{8,4},{12,8},{1,13},{5,1},{9,5},{13,9},{2,14},{6,2},{... | collective-permute-start | bytes 49160 | tf_op jit(solution)/shard_map/ppermute | solution.py:15
  153.0 1.0 copy-start.8
  153.0 1.0 copy-start.9
